TPU v7x, 256 devices: a whole 4x4x8 slice. The times are simulated.
256 devices in a mesh: tower: 16 (over z_lo, y, core), dev: 16 (over z_hi, x).
Axes of the slice: x: 4, y: 4, z: 8 (z_hi: 4, z_lo: 2; z = z_hi * 2 + z_lo), core: 2. Of those that a mesh axis runs over, the one named last changes fastest.
Arguments:
- bag_ids: int32 [16, 8192, 32, 4], P('tower', None, 'dev'), may hold values from 0 to 1023
- bag_lengths: int32 [16, 8192, 32], P('tower', None, 'dev'), may hold values from 1 to 4
- tables: bfloat16 [16, 32, 1024, 128], P('tower', 'dev'), may hold values from -3 to 3
- cross_down: bfloat16 [16, 1, 4096, 512], P('tower'), may hold values from -0.09375 to 0.09375
- cross_up: bfloat16 [16, 1, 512, 4096], P('tower'), may hold values from -0.25 to 0.25
- cross_bias: float32 [16, 1, 4096], P('tower'), may hold values from -4 to 4
- proj_weight: bfloat16 [16, 4096, 512], P('tower'), may hold values from -0.09375 to 0.09375
- proj_bias: float32 [16, 512], P('tower'), may hold values from -3 to 3
Outputs:
- interactions: float32 [8192, 120], P(('tower', 'dev'))
Inputs may be any that keep to these rules, and one draw needn't show every extreme that they name: `bag_ids`: where table rows travel between devices, each is sent as a whole 32-bit integer, one to a slot; a program may not pack several table rows into one word. `bag_lengths`: where bag lengths travel between devices, a program may pack several of them into one word.
All inputs are finite; a program needn't handle non-finite values.
Results may differ from a plain program's by a relative error of at most 0.0071.
Values may be sent and summed in bfloat16 or wider, within the bound.
A program may use at most 128 MiB of HBM per device.

v0:
```python
import jax
import jax.numpy as jnp
import numpy as np
from jax import lax
from jax.sharding import PartitionSpec as P

EMB = 128
OUT = 512


def pool_rows(tables_one, ids_one, lengths_one):
    table_rows = tables_one.shape[1]
    positions = lax.iota(jnp.int32, table_rows)
    counts = jnp.zeros(ids_one.shape[:2] + (table_rows,), jnp.bfloat16)
    for slot_index in range(ids_one.shape[2]):
        matched = (ids_one[:, :, slot_index, None] == positions) & (slot_index < lengths_one)[
            :, :, None
        ]
        counts = counts + matched.astype(jnp.bfloat16)
    summed = jnp.einsum("sft,ftd->sfd", counts, tables_one, preferred_element_type=jnp.float32)
    return summed.astype(jnp.bfloat16)


def tower_forward(base, down, up, bias, proj, proj_b):
    base_f = base.astype(jnp.float32)
    cross = base
    low = jnp.dot(cross, down[0], preferred_element_type=jnp.float32).astype(jnp.bfloat16)
    high = jnp.dot(low, up[0], preferred_element_type=jnp.float32) + bias[0]
    cross = (base_f * high + cross.astype(jnp.float32)).astype(jnp.bfloat16)
    return (jnp.dot(cross, proj, preferred_element_type=jnp.float32) + proj_b).astype(jnp.bfloat16)


def local(bag_ids, bag_lengths, tables, cross_down, cross_up, cross_bias, proj_weight, proj_bias):
    towers = lax.axis_size("tower")
    members = lax.axis_size("dev")
    samples = bag_ids.shape[1]
    block = samples // (towers * members)
    feat_dev = bag_ids.shape[2]
    slots = bag_ids.shape[3]
    weights = (cross_down[0], cross_up[0], cross_bias[0], proj_weight[0], proj_bias[0])
    every_table = lax.all_gather(tables[0], "dev", axis=0, tiled=True)
    keyed = bag_ids[0].reshape(towers, members, block, feat_dev, slots)
    counted = bag_lengths[0].reshape(towers, members, block, feat_dev)
    index = lax.all_to_all(keyed, "dev", split_axis=1, concat_axis=3, tiled=True)
    lengths_here = lax.all_to_all(counted, "dev", split_axis=1, concat_axis=3, tiled=True)
    count = index.shape[2]
    pooled = pool_rows(
        every_table,
        index.reshape(towers * count, -1, slots),
        lengths_here.reshape(towers * count, -1),
    )
    pooled_block = pooled.reshape(towers, 1, count, -1, EMB)
    finish_count = pooled_block.shape[2]
    rows = pooled_block.reshape(towers * finish_count, -1)
    outputs = tower_forward(rows, *weights).reshape(towers, finish_count, -1)
    gathered = lax.all_to_all(outputs, "tower", split_axis=0, concat_axis=0, tiled=True)
    gram = jnp.einsum(
        "isk,jsk->sij", gathered, gathered, preferred_element_type=jnp.float32
    ) / jnp.sqrt(jnp.float32(OUT))
    upper, lower = np.triu_indices(towers, 1)
    return gram[:, upper, lower]


def solution(mesh):
    placed = (
        P("tower", None, "dev", None),
        P("tower", None, "dev"),
        P("tower", "dev", None, None),
        P("tower", None, None, None),
        P("tower", None, None, None),
        P("tower", None, None),
        P("tower", None, None),
        P("tower", None),
    )
    return jax.shard_map(
        local, mesh=mesh, in_specs=placed, out_specs=P(("tower", "dev"), None), check_vma=False
    )
```

profile of v0, /device:TPU:1, one launch (start us, length us, event | category | flops | bytes accessed | tf_op | source)
XLA Modules:
  0.0 205.6 jit_solution(1138326824918847656)
XLA Ops:
  6.5 0.0 all-gather.3.cloned.1.call-start
  6.5 0.7 all-gather.3.cloned.1.call-update
  7.3 1.0 reshape_squeeze.7
  8.3 0.1 copy.47
  8.4 0.8 reshape.57
  9.1 11.6 %all-to-all-start.1 = ((s32[16,1,1024]{2,1,0:T(1,128)}), s32[16,1,1024]{2,1,0:T(1,128)S(1)}, u32[]{:S(2)}, u32[]{:S(2)}) async-start(s32[16,1,1024]{2,1,0:T(1,128)} %reshape.57), calls=%async_computation.1 | async-start | bytes 131072 | tf_op jit(solution)/shard_map/all_to_all | solution.py:45
  20.7 1.3 reshape_squeeze.6
  22.0 0.3 copy.46
  22.4 1.2 reshape.55
  23.5 6.1 %all-to-all-done.1 = s32[16,1,1024]{2,1,0:T(1,128)S(1)} async-done(((s32[16,1,1024]{2,1,0:T(1,128)}), s32[16,1,1024]{2,1,0:T(1,128)S(1)}, u32[]{:S(2)}, u32[]{:S(2)}) %all-to-all-start.1) | async-done | bytes 65568 | tf_op jit(solution)/shard_map/all_to_all | solution.py:45
  29.7 3.5 %all-to-all-start = ((s32[16,1,4096]{2,1,0:T(1,128)}), s32[16,1,4096]{2,1,0:T(1,128)S(1)}, u32[]{:S(2)}, u32[]{:S(2)}) async-start(s32[16,1,4096]{2,1,0:T(1,128)} %reshape.55), calls=%async_computation | async-start | bytes 524288 | tf_op jit(solution)/shard_map/all_to_all | solution.py:44
  33.2 0.5 broadcast.60
  33.7 0.8 reduce.1
  34.5 0.1 reshape.58
  34.6 0.1 compare_bitcast_fusion.3
  34.8 0.2 gt.80
  34.9 0.2 gt.95
  35.1 0.2 gt.90
  35.2 0.2 gt.85
  35.4 17.6 %all-to-all-done = s32[16,1,4096]{2,1,0:T(1,128)S(1)} async-done(((s32[16,1,4096]{2,1,0:T(1,128)}), s32[16,1,4096]{2,1,0:T(1,128)S(1)}, u32[]{:S(2)}, u32[]{:S(2)}) %all-to-all-start) | async-done | bytes 262176 | tf_op jit(solution)/shard_map/all_to_all | solution.py:44
  53.0 1.3 reduce
  54.2 0.3 reshape.56
  54.6 0.1 bitcast_bitcast_fusion
  54.7 0.1 copy.33
  54.8 0.4 reshape.46
  55.2 57.7 %fusion.53 = bf16[512,32,1024]{2,0,1:T(8,128)(2,1)} fusion(s32[512,32]{0,1:T(8,128)S(1)} %get-tuple-element.10, s32[512,32]{0,1:T(8,128)S(1)} %get-tuple-element.11, s32[512,32]{0,1:T(8,128)S(1)} %get-tuple-element.12, s32[512,32]{0,1:T(8,128)S(1)} %get-tuple-element.9, pred[512,32]{0,1:T(8,128)(4,1)S(1)} %gt.95, ...), kind=kLoop, calls=%fused_computation.13.clone.clone.clone.clone.1 | loop fusion | flops 335544320 | bytes 33882112 | tf_op jit(solution)/shard_map/sft,ftd->sfd/dot_general | solution.py:20
  113.0 14.5 %all-gather.3.cloned.1.call-done = bf16[1,32,1024,128]{3,2,0,1:T(8,128)(2,1)} async-done(((bf16[1,2,1024,128]{3,2,0,1:T(8,128)(2,1)}), bf16[1,32,1024,128]{3,2,0,1:T(8,128)(2,1)}) %all-gather.3.cloned.1.call-update) | async-done | bytes 8388624 | tf_op jit(solution)/shard_map/all_gather | solution.py:41
  127.5 18.9 %fusion.31 = bf16[32,512,128]{1,2,0:T(8,128)(2,1)} fusion(bf16[1,32,1024,128]{3,2,0,1:T(8,128)(2,1)} %all-gather.3.cloned.1.call-done, bf16[512,32,1024]{2,0,1:T(8,128)(2,1)} %fusion.53), kind=kOutput, calls=%fused_computation.33 | convolution fusion | flops 4297064448 | bytes 46137344 | tf_op jit(solution)/shard_map/sft,ftd->sfd/dot_general | solution.py:20
  146.3 0.0 copy-start.1
  146.3 6.4 %copy.37 = bf16[512,4096]{1,0:T(8,128)(2,1)} copy(bf16[512,4096]{0,1:T(8,128)(2,1)} %bitcast.98) | data formatting | bytes 8388608 | tf_op jit(solution)/shard_map/reshape;reshape | solution.py:54
  152.8 0.0 copy-done.1
  152.8 0.0 copy-start.2
  152.8 12.7 %fusion.24 = bf16[512,4096]{1,0:T(8,128)(2,1)} fusion(bf16[512,4096]{1,0:T(8,128)(2,1)} %copy.37, bf16[1,1,512,4096]{3,2,1,0:T(8,128)(2,1)} %param.16, f32[4096]{0:T(1024)S(1)} %bitcast.104, bf16[512,4096]{0,1:T(8,128)(2,1)} %bitcast.99, bf16[1,1,4096,512]{3,2,1,0:T(8,128)(2,1)} %param.15), kind=kOutput, calls=%fused_computation.26 | convolution fusion | flops 4305715200 | bytes 20987904 | tf_op jit(solution)/shard_map/dot_general | solution.py:28
  165.5 0.0 copy-done.2
  165.5 0.0 copy-start
  165.5 5.8 %fusion.39 = bf16[512,512]{1,0:T(8,128)(2,1)S(1)} fusion(bf16[512,4096]{1,0:T(8,128)(2,1)} %fusion.24, bf16[1,4096,512]{2,1,0:T(8,128)(2,1)} %param.18, f32[512]{0:T(512)S(1)} %bitcast.105), kind=kOutput, calls=%fused_computation.35 | convolution fusion | flops 2148007936 | bytes 8914944 | tf_op jit(solution)/shard_map/dot_general | solution.py:30
  171.3 24.6 %all_to_all.29 = bf16[16,32,512]{2,1,0:T(8,128)(2,1)S(1)} all-to-all(bf16[16,32,512]{2,1,0:T(8,128)(2,1)S(1)} %bitcast.102), channel_id=1, replica_groups=mesh['tower'=16,'dev'=16] {'tower'}, dimensions={0} | all-to-all | bytes 1048576 | tf_op jit(solution)/shard_map/all_to_all | solution.py:56
  195.9 0.4 convolution_multiply_fusion
  196.3 0.2 copy.40
  196.5 0.0 copy-done
  196.5 1.6 gather_fusion
  198.1 0.7 copy.41
  (1 shorter events, 0.0 us)
Async XLA Ops:
  6.5 120.9 %all-gather.3.cloned.1.call-start = ((), (), s32[]{:S(2)}) async-start(), calls=%async_computation.3 | async-start | bytes 8912896 | tf_op jit(solution)/shard_map/all_gather | solution.py:41
  9.1 20.5 %all-to-all-start.1 = ((s32[16,1,1024]{2,1,0:T(1,128)}), s32[16,1,1024]{2,1,0:T(1,128)S(1)}, u32[]{:S(2)}, u32[]{:S(2)}) async-start(s32[16,1,1024]{2,1,0:T(1,128)} %reshape.57), calls=%async_computation.1 | async-start | bytes 131072 | tf_op jit(solution)/shard_map/all_to_all | solution.py:45
  29.7 23.3 %all-to-all-start = ((s32[16,1,4096]{2,1,0:T(1,128)}), s32[16,1,4096]{2,1,0:T(1,128)S(1)}, u32[]{:S(2)}, u32[]{:S(2)}) async-start(s32[16,1,4096]{2,1,0:T(1,128)} %reshape.55), calls=%async_computation | async-start | bytes 524288 | tf_op jit(solution)/shard_map/all_to_all | solution.py:44
  146.3 6.5 %copy-start.1 = (f32[1,1,4096]{2,1,0:T(1,128)S(1)}, f32[1,1,4096]{2,1,0:T(1,128)}, u32[]{:S(2)}) copy-start(f32[1,1,4096]{2,1,0:T(1,128)} %param.17) | copy-start | bytes 49156
  152.8 12.7 %copy-start.2 = (f32[1,512]{1,0:T(1,128)S(1)}, f32[1,512]{1,0:T(1,128)}, u32[]{:S(2)}) copy-start(f32[1,512]{1,0:T(1,128)} %param.19) | copy-start | bytes 6148
  165.5 31.0 %copy-start = (s32[120]{0:T(128)S(1)}, s32[120]{0:T(128)}, u32[]{:S(2)}) copy-start(s32[120]{0:T(128)} %constant.53) | copy-start | bytes 1444
Sparse Core Ops, SparseCore 0:
  9.8 117.6 all-gather.2
where the time goes:
time: 206 us
  other arithmetic  59.9 us (29%)
  waiting for transfers between devices  38.9 us (19%)
  matrix products  37.8 us (18%)
  blocking collectives  24.6 us (12%)
  local copies, waits for them, and re-layouts  15.8 us (8%)
  starting transfers between devices  15.1 us (7%)
  between operations  13.5 us (7%)
    dot_general x1, other arithmetic, pool_rows(): jnp.einsum('sft,ftd->sfd', counts, tables_one, preferred_element_type=jnp...  57.7 us
    all_to_all x1, blocking collectives, local(): lax.all_to_all(outputs, 'tower', split_axis=0, concat_axis=0, tiled=True)  24.6 us
    dot_general x1, matrix products, pool_rows(): jnp.einsum('sft,ftd->sfd', counts, tables_one, preferred_element_type=jnp...  18.9 us
    all_to_all x1, waiting for transfers between devices, local(): lax.all_to_all(keyed, 'dev', split_axis=1, concat_axis=3, tiled=True)  17.6 us
    all_gather x1, waiting for transfers between devices, local(): every_table = lax.all_gather(tables[0], 'dev', axis=0, tiled=True)  14.5 us
    dot_general x1, matrix products, tower_forward(): high = jnp.dot(low, up[0], preferred_element_type=jnp.float32) + bias[0]  12.7 us
    all_to_all x1, starting transfers between devices, local(): lax.all_to_all(counted, 'dev', split_axis=1, concat_axis=3, tiled=True)  11.6 us
    another operation x1, local copies, waits for them, and re-layouts, local(): rows = pooled_block.reshape(towers * finish_count, -1)  6.45 us
  transfers between devices with their start and end apart: 3, of which 3 were waited for; matrix products, arithmetic and copies ran while one was open for 32% of the time, Pallas kernels for 0%

commit v1 on v0

--- a/solution.py
+++ b/solution.py
@@ -38,7 +38,11 @@
     feat_dev = bag_ids.shape[2]
     slots = bag_ids.shape[3]
     weights = (cross_down[0], cross_up[0], cross_bias[0], proj_weight[0], proj_bias[0])
-    every_table = lax.all_gather(tables[0], "dev", axis=0, tiled=True)
+    own = tables[0]
+    size = lax.axis_size("dev")
+    pieces = jnp.stack([own for _ in range(size)])
+    pieces = lax.all_to_all(pieces, "dev", split_axis=0, concat_axis=0)
+    every_table = jnp.concatenate(pieces, axis=0)
     keyed = bag_ids[0].reshape(towers, members, block, feat_dev, slots)
     counted = bag_lengths[0].reshape(towers, members, block, feat_dev)
     index = lax.all_to_all(keyed, "dev", split_axis=1, concat_axis=3, tiled=True)

time: 206 us -> 302 us (1.47)
  waiting for transfers between devices: 38.9 us -> 141 us
  between operations: 13.5 us -> 0.14 us
  local copies, waits for them, and re-layouts: 15.8 us -> 21.2 us
  starting transfers between devices: 15.1 us -> 20 us
  blocking collectives: 24.6 us -> 20.3 us
    all_to_all x0 -> x1, waiting for transfers between devices: none -> 126 us  [local(): pieces = lax.all_to_all(pieces, 'dev', split_axis=0, concat_axis=0)]
    all_gather x1 -> x0, waiting for transfers between devices: 14.5 us -> none  [local(): every_table = lax.all_gather(tables[0], 'dev', axis=0, tiled=True)]
    all_to_all x1, waiting for transfers between devices: 17.6 us -> 8.91 us  [local(): lax.all_to_all(keyed, 'dev', split_axis=1, concat_axis=3, tiled=True)]
    another operation x0 -> x2, local copies, waits for them, and re-layouts: none -> 5.52 us  [the longest x1 4.28 us: local(): pieces = jnp.stack([own for _ in range(size)])]
    all_to_all x0 -> x1, starting transfers between devices: none -> 4.94 us  [local(): pieces = lax.all_to_all(pieces, 'dev', split_axis=0, concat_axis=0)]
    all_to_all x1, blocking collectives: 24.6 us -> 20.3 us  [local(): lax.all_to_all(outputs, 'tower', split_axis=0, concat_axis=0, tiled=True)]
  transfers between devices with their start and end apart: 3 -> 3, of which waited for: 3 -> 3; matrix products, arithmetic and copies ran while one was open for 32% -> 22% of each run, Pallas kernels for 0% -> 0%
where the time goes in v1:
time: 302 us
  waiting for transfers between devices  141 us (47%)
  other arithmetic  59.9 us (20%)
  matrix products  38.6 us (13%)
  local copies, waits for them, and re-layouts  21.2 us (7%)
  blocking collectives  20.3 us (7%)
  starting transfers between devices  20 us (7%)
    all_to_all x1, waiting for transfers between devices, local(): pieces = lax.all_to_all(pieces, 'dev', split_axis=0, concat_axis=0)  126 us
    dot_general x1, other arithmetic, pool_rows(): jnp.einsum('sft,ftd->sfd', counts, tables_one, preferred_element_type=jnp...  57.7 us
    all_to_all x1, blocking collectives, local(): lax.all_to_all(outputs, 'tower', split_axis=0, concat_axis=0, tiled=True)  20.3 us
    dot_general x1, matrix products, pool_rows(): jnp.einsum('sft,ftd->sfd', counts, tables_one, preferred_element_type=jnp...  19.7 us
    dot_general x1, matrix products, tower_forward(): high = jnp.dot(low, up[0], preferred_element_type=jnp.float32) + bias[0]  12.7 us
    all_to_all x1, starting transfers between devices, local(): lax.all_to_all(counted, 'dev', split_axis=1, concat_axis=3, tiled=True)  11.6 us
    all_to_all x1, waiting for transfers between devices, local(): lax.all_to_all(keyed, 'dev', split_axis=1, concat_axis=3, tiled=True)  8.91 us
    another operation x1, local copies, waits for them, and re-layouts, local(): rows = pooled_block.reshape(towers * finish_count, -1)  6.4 us
  transfers between devices with their start and end apart: 3, of which 3 were waited for; matrix products, arithmetic and copies ran while one was open for 22% of the time, Pallas kernels for 0%

profile of v1, /device:TPU:1, one launch (start us, length us, event | category | flops | bytes accessed | tf_op | source)
XLA Modules:
  0.0 301.6 jit_solution(15151791337683636980)
XLA Ops:
  0.0 1.0 reshape_squeeze.7
  1.0 0.1 copy.45
  1.1 0.8 reshape.61
  1.9 11.6 %all-to-all-start.1 = ((s32[16,1,1024]{2,1,0:T(1,128)}), s32[16,1,1024]{2,1,0:T(1,128)S(1)}, u32[]{:S(2)}, u32[]{:S(2)}) async-start(s32[16,1,1024]{2,1,0:T(1,128)} %reshape.61), calls=%async_computation.1 | async-start | bytes 131072 | tf_op jit(solution)/shard_map/all_to_all | solution.py:49
  13.5 1.3 reshape_squeeze.6
  14.8 0.3 copy.44
  15.1 1.2 reshape.59
  16.3 6.1 %all-to-all-done.1 = s32[16,1,1024]{2,1,0:T(1,128)S(1)} async-done(((s32[16,1,1024]{2,1,0:T(1,128)}), s32[16,1,1024]{2,1,0:T(1,128)S(1)}, u32[]{:S(2)}, u32[]{:S(2)}) %all-to-all-start.1) | async-done | bytes 65568 | tf_op jit(solution)/shard_map/all_to_all | solution.py:49
  22.4 3.5 %all-to-all-start = ((s32[16,1,4096]{2,1,0:T(1,128)}), s32[16,1,4096]{2,1,0:T(1,128)S(1)}, u32[]{:S(2)}, u32[]{:S(2)}) async-start(s32[16,1,4096]{2,1,0:T(1,128)} %reshape.59), calls=%async_computation | async-start | bytes 524288 | tf_op jit(solution)/shard_map/all_to_all | solution.py:48
  25.9 1.2 copy.34
  27.2 8.9 %all-to-all-done = s32[16,1,4096]{2,1,0:T(1,128)S(1)} async-done(((s32[16,1,4096]{2,1,0:T(1,128)}), s32[16,1,4096]{2,1,0:T(1,128)S(1)}, u32[]{:S(2)}, u32[]{:S(2)}) %all-to-all-start) | async-done | bytes 262176 | tf_op jit(solution)/shard_map/all_to_all | solution.py:48
  36.1 4.3 %stack.3 = bf16[16,2,1024,128]{2,3,1,0:T(8,128)(2,1)} broadcast(bf16[2,1024,128]{1,2,0:T(8,128)(2,1)S(1)} %copy.34), dimensions={1,2,3} | broadcast | bytes 8912896 | tf_op jit(solution)/shard_map/stack | solution.py:43
  40.4 4.9 %all-to-all-start.2 = ((bf16[16,2,1024,128]{2,3,1,0:T(8,128)(2,1)}), bf16[16,2,1024,128]{2,3,1,0:T(8,128)(2,1)}, u32[]{:S(2)}, u32[]{:S(2)}) async-start(bf16[16,2,1024,128]{2,3,1,0:T(8,128)(2,1)} %stack.3), calls=%async_computation.2 | async-start | bytes 16777216 | tf_op jit(solution)/shard_map/all_to_all | solution.py:44
  45.3 0.5 broadcast.61
  45.8 0.8 reduce.1
  46.7 0.1 reshape.62
  46.8 0.1 compare_bitcast_fusion.3
  46.9 0.2 gt.80
  47.1 0.2 gt.95
  47.2 0.2 gt.90
  47.4 0.2 gt.85
  47.5 1.3 reduce
  48.8 0.3 reshape.60
  49.2 0.1 bitcast_bitcast_fusion
  49.3 0.1 copy.32
  49.3 0.4 reshape.50
  49.8 57.7 %fusion.51 = bf16[512,32,1024]{2,0,1:T(8,128)(2,1)} fusion(s32[512,32]{0,1:T(8,128)S(1)} %get-tuple-element.10, s32[512,32]{0,1:T(8,128)S(1)} %get-tuple-element.11, s32[512,32]{0,1:T(8,128)S(1)} %get-tuple-element.12, s32[512,32]{0,1:T(8,128)S(1)} %get-tuple-element.9, pred[512,32]{0,1:T(8,128)(4,1)S(1)} %gt.95, ...), kind=kLoop, calls=%fused_computation.13.clone.clone.clone.clone.1 | loop fusion | flops 335544320 | bytes 33882112 | tf_op jit(solution)/shard_map/sft,ftd->sfd/dot_general | solution.py:20
  107.5 126.4 %all-to-all-done.2 = bf16[16,2,1024,128]{2,3,1,0:T(8,128)(2,1)} async-done(((bf16[16,2,1024,128]{2,3,1,0:T(8,128)(2,1)}), bf16[16,2,1024,128]{2,3,1,0:T(8,128)(2,1)}, u32[]{:S(2)}, u32[]{:S(2)}) %all-to-all-start.2) | async-done | bytes 8388640 | tf_op jit(solution)/shard_map/all_to_all | solution.py:44
  233.9 19.7 %fusion.30 = bf16[32,512,128]{1,2,0:T(8,128)(2,1)} fusion(bf16[32,1024,128]{1,2,0:T(8,128)(2,1)} %bitcast.15, bf16[512,32,1024]{2,0,1:T(8,128)(2,1)} %fusion.51), kind=kOutput, calls=%fused_computation.32 | convolution fusion | flops 4297064448 | bytes 46137344 | tf_op jit(solution)/shard_map/sft,ftd->sfd/dot_general | solution.py:20
  253.6 0.0 copy-start.1
  253.6 6.4 %copy.35 = bf16[512,4096]{1,0:T(8,128)(2,1)} copy(bf16[512,4096]{0,1:T(8,128)(2,1)} %bitcast.94) | data formatting | bytes 8388608 | tf_op jit(solution)/shard_map/reshape;reshape | solution.py:58
  260.0 0.0 copy-done.1
  260.0 0.0 copy-start.2
  260.0 12.7 %fusion.24 = bf16[512,4096]{1,0:T(8,128)(2,1)} fusion(bf16[512,4096]{1,0:T(8,128)(2,1)} %copy.35, bf16[1,1,512,4096]{3,2,1,0:T(8,128)(2,1)} %param.16, f32[4096]{0:T(1024)S(1)} %bitcast.100, bf16[512,4096]{0,1:T(8,128)(2,1)} %bitcast.95, bf16[1,1,4096,512]{3,2,1,0:T(8,128)(2,1)} %param.15), kind=kOutput, calls=%fused_computation.26 | convolution fusion | flops 4305715200 | bytes 20987904 | tf_op jit(solution)/shard_map/dot_general | solution.py:28
  272.7 0.0 copy-done.2
  272.7 0.0 copy-start
  272.7 5.8 %fusion.36 = bf16[512,512]{1,0:T(8,128)(2,1)S(1)} fusion(bf16[512,4096]{1,0:T(8,128)(2,1)} %fusion.24, bf16[1,4096,512]{2,1,0:T(8,128)(2,1)} %param.18, f32[512]{0:T(512)S(1)} %bitcast.101), kind=kOutput, calls=%fused_computation.34 | convolution fusion | flops 2148007936 | bytes 8914944 | tf_op jit(solution)/shard_map/dot_general | solution.py:30
  278.5 20.3 %all_to_all.34 = bf16[16,32,512]{2,1,0:T(8,128)(2,1)S(1)} all-to-all(bf16[16,32,512]{2,1,0:T(8,128)(2,1)S(1)} %bitcast.98), channel_id=1, replica_groups=mesh['tower'=16,'dev'=16] {'tower'}, dimensions={0} | all-to-all | bytes 1048576 | tf_op jit(solution)/shard_map/all_to_all | solution.py:60
  298.8 0.4 convolution_multiply_fusion
  299.2 0.2 copy.38
  299.4 0.0 copy-done
  299.4 1.6 gather_fusion
  301.0 0.7 copy.39
  (1 shorter events, 0.0 us)
Async XLA Ops:
  1.9 20.5 %all-to-all-start.1 = ((s32[16,1,1024]{2,1,0:T(1,128)}), s32[16,1,1024]{2,1,0:T(1,128)S(1)}, u32[]{:S(2)}, u32[]{:S(2)}) async-start(s32[16,1,1024]{2,1,0:T(1,128)} %reshape.61), calls=%async_computation.1 | async-start | bytes 131072 | tf_op jit(solution)/shard_map/all_to_all | solution.py:49
  22.4 13.7 %all-to-all-start = ((s32[16,1,4096]{2,1,0:T(1,128)}), s32[16,1,4096]{2,1,0:T(1,128)S(1)}, u32[]{:S(2)}, u32[]{:S(2)}) async-start(s32[16,1,4096]{2,1,0:T(1,128)} %reshape.59), calls=%async_computation | async-start | bytes 524288 | tf_op jit(solution)/shard_map/all_to_all | solution.py:48
  40.4 193.5 %all-to-all-start.2 = ((bf16[16,2,1024,128]{2,3,1,0:T(8,128)(2,1)}), bf16[16,2,1024,128]{2,3,1,0:T(8,128)(2,1)}, u32[]{:S(2)}, u32[]{:S(2)}) async-start(bf16[16,2,1024,128]{2,3,1,0:T(8,128)(2,1)} %stack.3), calls=%async_computation.2 | async-start | bytes 16777216 | tf_op jit(solution)/shard_map/all_to_all | solution.py:44
  253.6 6.4 %copy-start.1 = (f32[1,1,4096]{2,1,0:T(1,128)S(1)}, f32[1,1,4096]{2,1,0:T(1,128)}, u32[]{:S(2)}) copy-start(f32[1,1,4096]{2,1,0:T(1,128)} %param.17) | copy-start | bytes 49156
  260.0 12.7 %copy-start.2 = (f32[1,512]{1,0:T(1,128)S(1)}, f32[1,512]{1,0:T(1,128)}, u32[]{:S(2)}) copy-start(f32[1,512]{1,0:T(1,128)} %param.19) | copy-start | bytes 6148
  272.7 26.6 %copy-start = (s32[120]{0:T(128)S(1)}, s32[120]{0:T(128)}, u32[]{:S(2)}) copy-start(s32[120]{0:T(128)} %constant.53) | copy-start | bytes 1444
